TPU v7x, 32 devices: a whole 2x2x4 slice. The times are simulated.
32 devices in a mesh: groups: 2 (over y), seq: 4 (over x, core), chan: 4 (over z).
Axes of the slice: x: 2, y: 2, z: 4, core: 2. Of those that a mesh axis runs over, the one named last changes fastest.
Arguments:
- tokens: bfloat16 [4096, 4096], P(('groups', 'seq'), 'chan'), parts along dimension 0, may hold values from -6 to 6
- norm_gain: float32 [4096], replicated, may hold values from 0.5 to 1.5
- proj_weight: bfloat16 [4096, 3, 4096], P('seq', None, 'chan'), may hold values from -0.09375 to 0.09375
- short_filter: float32 [3, 3, 4096], P(None, None, 'chan'), may hold values from -2.5 to 2.5
- long_filter: float32 [4096, 2048], P('chan', 'seq'), may hold values from -4 to 4, as said below
- skip_gain: float32 [4096], P('chan'), may hold values from 0.5 to 1.5
- out_weight: bfloat16 [4096, 4096], P(None, 'chan'), may hold values from -0.09375 to 0.09375
Outputs:
- block_out: bfloat16 [4096, 4096], P(('groups', 'seq'), 'chan'), parts along dimension 0
There are 2 independent parts, one for each index of `groups`. A program takes and returns all parts, laid end to end along the dimension named above; an argument that names none is the same for every part. Nothing has to cross between parts.
Inputs may be any that keep to these rules, and one draw needn't show every extreme that they name: `long_filter`: filter taps of the sequence-long convolution.
All inputs are finite; a program needn't handle non-finite values.
Results may differ from a plain program's by a relative error of at most 0.012.
Values may be sent and summed in bfloat16 or wider, within the bound.
A program may use at most 128 MiB of HBM per device.

v0:
```python
import math
import jax
import jax.numpy as jnp
from jax import lax
from jax.sharding import PartitionSpec as P

SHORT = 3
EPSILON = 1e-06
HIGHEST = lax.Precision.HIGHEST


def from_behind(value, axis, steps):
    count = lax.axis_size(axis)
    initial, last = (max(0, -steps), min(count, count - steps))
    return lax.ppermute(value, axis, [(source, source + steps) for source in range(initial, last)])


def angle_table(row_count, col_count, period, sign):
    row_index = lax.iota(jnp.int32, row_count)[:, None]
    col_index = lax.iota(jnp.int32, col_count)[None, :]
    angles = (row_index * col_index % period).astype(jnp.float32) * (sign * 2.0 * math.pi / period)
    return (jnp.cos(angles), jnp.sin(angles))


def forward_spectrum(signal_rows, first, second):
    channels = signal_rows.shape[0]
    grid_rows = signal_rows.reshape(channels, first, second)
    cos_first, sin_first = angle_table(first, first, first, -1.0)
    part_re = jnp.einsum("cab,ak->ckb", grid_rows, cos_first, precision=HIGHEST)
    part_im = jnp.einsum("cab,ak->ckb", grid_rows, sin_first, precision=HIGHEST)
    twist_cos, twist_sin = angle_table(first, second, first * second, -1.0)
    part_re, part_im = (
        part_re * twist_cos - part_im * twist_sin,
        part_re * twist_sin + part_im * twist_cos,
    )
    cos_second, sin_second = angle_table(second, second, second, -1.0)
    spectrum_real = jnp.einsum("ckb,bm->ckm", part_re, cos_second, precision=HIGHEST) - jnp.einsum(
        "ckb,bm->ckm", part_im, sin_second, precision=HIGHEST
    )
    spec_im = jnp.einsum("ckb,bm->ckm", part_re, sin_second, precision=HIGHEST) + jnp.einsum(
        "ckb,bm->ckm", part_im, cos_second, precision=HIGHEST
    )
    return (spectrum_real, spec_im)


def inverse_spectrum(spectrum_real, spec_im, first, second):
    channels = spectrum_real.shape[0]
    cos_second, sin_second = angle_table(second, second, second, 1.0)
    part_re = jnp.einsum("ckm,bm->ckb", spectrum_real, cos_second, precision=HIGHEST) - jnp.einsum(
        "ckm,bm->ckb", spec_im, sin_second, precision=HIGHEST
    )
    part_im = jnp.einsum("ckm,bm->ckb", spectrum_real, sin_second, precision=HIGHEST) + jnp.einsum(
        "ckm,bm->ckb", spec_im, cos_second, precision=HIGHEST
    )
    twist_cos, twist_sin = angle_table(first, second, first * second, 1.0)
    part_re, part_im = (
        part_re * twist_cos - part_im * twist_sin,
        part_re * twist_sin + part_im * twist_cos,
    )
    cos_first, sin_first = angle_table(first, first, first, 1.0)
    result = jnp.einsum("ckb,ak->cab", part_re, cos_first, precision=HIGHEST) - jnp.einsum(
        "ckb,ak->cab", part_im, sin_first, precision=HIGHEST
    )
    return result.reshape(channels, first * second) / (first * second)


def spectral_conv(signal_rows, filter_rows):
    channels, length = signal_rows.shape
    padded_len = 2 * length
    log_len = padded_len.bit_length() - 1
    first = 1 << log_len // 2
    second = padded_len // first
    zeros_tail = jnp.zeros((channels, length), jnp.float32)
    sig_re, sig_im = forward_spectrum(
        jnp.concatenate([signal_rows, zeros_tail], axis=1), first, second
    )
    tap_re, tap_im = forward_spectrum(
        jnp.concatenate([filter_rows, zeros_tail], axis=1), first, second
    )
    prod_re = sig_re * tap_re - sig_im * tap_im
    prod_im = sig_re * tap_im + sig_im * tap_re
    return inverse_spectrum(prod_re, prod_im, first, second)[:, :length]


def short_filter_output(projected, rim_cells, kernel_coefficients):
    count = kernel_coefficients.shape[0]
    steps_len = projected.shape[2]
    extended = jnp.concatenate([rim_cells, projected], axis=2).astype(jnp.float32)
    total = jnp.zeros(projected.shape, jnp.float32)
    for tap in range(count):
        total = (
            total
            + kernel_coefficients[tap][:, :, None]
            * extended[:, :, count - 1 - tap : count - 1 - tap + steps_len]
        )
    return total.astype(jnp.bfloat16)


def hyena_mixer(keys_rows, values_rows, long_taps, skip_part):
    middle = keys_rows.astype(jnp.float32) * values_rows.astype(jnp.float32)
    return (spectral_conv(middle, long_taps) + skip_part[:, None] * middle).astype(jnp.bfloat16)


def body(tokens, norm_gain, proj_weight, short_filter, long_filter, skip_gain, out_weight):
    seq_count = lax.axis_size("seq")
    local_rows = tokens.shape[0]
    local_chan = proj_weight.shape[2]
    subset = local_chan // seq_count
    length = local_rows * seq_count
    offset = lax.axis_index("seq") * subset
    whole = lax.all_gather(tokens, "chan", axis=1, tiled=True)
    wide = whole.astype(jnp.float32)
    rescaled_signal = (
        wide * lax.rsqrt(jnp.mean(wide * wide, axis=1, keepdims=True) + EPSILON) * norm_gain
    ).astype(jnp.bfloat16)
    projected = lax.dot_general(
        lax.all_gather(proj_weight, "seq", axis=0, tiled=True),
        rescaled_signal,
        (((0,), (1,)), ((), ())),
        preferred_element_type=jnp.float32,
    ).astype(jnp.bfloat16)
    taps_grid = long_filter.reshape(1, seq_count, subset, local_rows)
    long_taps = lax.all_to_all(taps_grid, "seq", split_axis=1, concat_axis=3, tiled=True).reshape(
        subset, length
    )
    skip_part = lax.dynamic_slice_in_dim(skip_gain, offset, subset, 0)
    rim_cells = from_behind(projected[:, :, local_rows - (SHORT - 1) :], "seq", 1)
    featured = short_filter_output(projected, rim_cells, short_filter)
    pair_grid = featured[1:].reshape(2, seq_count, subset, local_rows)
    moved = lax.all_to_all(pair_grid, "seq", split_axis=1, concat_axis=3, tiled=True).reshape(
        2, subset, length
    )
    result = hyena_mixer(moved[0], moved[1], long_taps, skip_part)
    returned = lax.all_to_all(
        result.reshape(1, subset, length), "seq", split_axis=2, concat_axis=0, tiled=True
    )
    returned = returned.reshape(local_chan, local_rows)
    gated = (featured[0].astype(jnp.float32) * returned.astype(jnp.float32)).astype(jnp.bfloat16)
    full_mix = lax.all_gather(gated, "chan", axis=0, tiled=True)
    update = lax.dot_general(
        full_mix, out_weight, (((0,), (0,)), ((), ())), preferred_element_type=jnp.float32
    )
    return (tokens.astype(jnp.float32) + update).astype(jnp.bfloat16)


def solution(mesh):
    placed = (
        P(("groups", "seq"), "chan"),
        P(),
        P("seq", None, "chan"),
        P(None, None, "chan"),
        P("chan", "seq"),
        P("chan"),
        P(None, "chan"),
    )
    return jax.shard_map(
        body, mesh=mesh, in_specs=placed, out_specs=P(("groups", "seq"), "chan"), check_vma=False
    )
```

profile of v0, /device:TPU:0, one launch (start us, length us, event | category | flops | bytes accessed | tf_op | source)
XLA Modules:
  0.0 568.1 jit_solution(13785095065940686060)
XLA Ops:
  12.3 80.1 %all-gather.4.cloned.1.call-done = bf16[512,4096]{1,0:T(8,128)(2,1)} async-done(((bf16[512,1024]{1,0:T(8,128)(2,1)}), bf16[512,4096]{1,0:T(8,128)(2,1)}) %all-gather.4.cloned.1.call-update) | async-done | bytes 4194320 | tf_op jit(solution)/shard_map/all_gather | solution.py:111
  95.5 151.8 %all-gather.6.cloned.1.call-done = bf16[4096,3,1024]{2,0,1:T(8,128)(2,1)} async-done(((bf16[1024,3,1024]{2,0,1:T(8,128)(2,1)}), bf16[4096,3,1024]{2,0,1:T(8,128)(2,1)}) %all-gather.6.cloned.1.call-update) | async-done | bytes 25165840 | tf_op jit(solution)/shard_map/all_gather | solution.py:117
  247.3 18.2 %convert_bitcast_fusion = bf16[3,1024,512]{1,2,0:T(8,128)(2,1)S(1)} fusion(bf16[4096,3,1024]{2,0,1:T(8,128)(2,1)} %all-gather.6.cloned.1.call-done, bf16[512,4096]{1,0:T(8,128)(2,1)} %all-gather.4.cloned.1.call-done, f32[4096]{0:T(1024)S(1)} %copy-done.5, f32[512]{0:T(512)S(1)} %add_rsqrt_fusion), kind=kOutput, calls=%fused_computation.53 | convolution fusion | flops 12894863360 | bytes 32524288 | tf_op jit(solution)/shard_map/dot_general | solution.py:116
  283.4 7.2 %fusion.23 = f32[64,256,64]{1,0,2:T(8,128)} fusion(f32[256,64,64]{0,2,1:T(8,128)S(1)} %bitcast.128), kind=kOutput, calls=%fused_computation.36 | convolution fusion | flops 805363712 | bytes 8388608 | tf_op jit(solution)/shard_map/cab,ak->ckb/dot_general | solution.py:30
  290.6 7.2 %fusion.25 = f32[64,256,64]{1,0,2:T(8,128)} fusion(f32[256,64,64]{0,2,1:T(8,128)S(1)} %bitcast.129), kind=kOutput, calls=%fused_computation.38 | convolution fusion | flops 805363712 | bytes 8388608 | tf_op jit(solution)/shard_map/cab,ak->ckb/dot_general | solution.py:29
  297.7 7.3 %all-to-all-done = bf16[2,4,256,512]{2,3,0,1:T(8,128)(2,1)} async-done(((bf16[2,4,256,512]{2,3,0,1:T(8,128)(2,1)}), bf16[2,4,256,512]{2,3,0,1:T(8,128)(2,1)}, u32[]{:S(2)}, u32[]{:S(2)}) %all-to-all-start) | async-done | bytes 2097184 | tf_op jit(solution)/shard_map/all_to_all | solution.py:130
  309.2 7.1 %fusion.35 = f32[64,256,64]{1,0,2:T(8,128)} fusion(f32[256,64,64]{0,2,1:T(8,128)S(1)} %bitcast.130), kind=kOutput, calls=%fused_computation.48 | convolution fusion | flops 805363712 | bytes 8388608 | tf_op jit(solution)/shard_map/cab,ak->ckb/dot_general | solution.py:30
  316.3 12.5 %subtract_bitcast_fusion = (f32[256,64,64]{0,1,2:T(8,128)S(1)}, f32[256,64,64]{0,1,2:T(8,128)S(1)}, f32[256,64,64]{0,1,2:T(8,128)S(1)}, f32[256,64,64]{0,1,2:T(8,128)S(1)}) fusion(f32[64,256,64]{1,0,2:T(8,128)} %fusion.23, f32[64,256,64]{1,0,2:T(8,128)} %fusion.25, f32[64,64]{0,1:T(8,128)S(1)} %copy.102, f32[64,64]{0,1:T(8,128)S(1)} %copy.99, ...), kind=kOutput, calls=%fused_computation.23 | convolution fusion | flops 817946624 | bytes 33587200 | tf_op jit(solution)/shard_map/cab,ak->ckb/dot_general | solution.py:29
  328.8 6.5 %fusion.15 = f32[256,64,64]{0,2,1:T(8,128)S(1)} fusion(f32[256,64,64]{0,1,2:T(8,128)S(1)} %get-tuple-element.10), kind=kOutput, calls=%fused_computation.28 | convolution fusion | flops 805363712 | bytes 8388608 | tf_op jit(solution)/shard_map/ckb,bm->ckm/dot_general | solution.py:40
  335.3 6.9 %fusion.17 = f32[256,64,64]{0,2,1:T(8,128)S(1)} fusion(f32[256,64,64]{0,1,2:T(8,128)S(1)} %get-tuple-element.10), kind=kOutput, calls=%fused_computation.30 | convolution fusion | flops 805363712 | bytes 8388608 | tf_op jit(solution)/shard_map/ckb,bm->ckm/dot_general | solution.py:37
  342.3 7.3 %fusion.27 = f32[256,64,64]{0,2,1:T(8,128)} fusion(f32[256,64,64]{0,1,2:T(8,128)S(1)} %get-tuple-element.13), kind=kOutput, calls=%fused_computation.40 | convolution fusion | flops 805363712 | bytes 8388608 | tf_op jit(solution)/shard_map/ckb,bm->ckm/dot_general | solution.py:40
  349.6 6.5 %fusion.29 = f32[256,64,64]{0,2,1:T(8,128)S(1)} fusion(f32[256,64,64]{0,1,2:T(8,128)S(1)} %get-tuple-element.13), kind=kOutput, calls=%fused_computation.42 | convolution fusion | flops 805363712 | bytes 8388608 | tf_op jit(solution)/shard_map/ckb,bm->ckm/dot_general | solution.py:37
  356.1 7.3 %fusion.47 = f32[256,64,64]{0,2,1:T(8,128)S(1)} fusion(f32[256,64,64]{0,2,1:T(8,128)S(1)} %fusion.17, f32[256,64,64]{0,1,2:T(8,128)S(1)} %get-tuple-element.9), kind=kOutput, calls=%fused_computation.56 | convolution fusion | flops 806412288 | bytes 12582912 | tf_op jit(solution)/shard_map/ckb,bm->ckm/dot_general | solution.py:37
  363.3 7.4 %fusion.50 = f32[256,64,64]{0,2,1:T(8,128)} fusion(f32[256,64,64]{0,2,1:T(8,128)S(1)} %fusion.15, f32[256,64,64]{0,1,2:T(8,128)S(1)} %get-tuple-element.9), kind=kOutput, calls=%fused_computation.57 | convolution fusion | flops 806412288 | bytes 12582912 | tf_op jit(solution)/shard_map/ckb,bm->ckm/dot_general | solution.py:40
  370.7 7.4 %fusion.41 = f32[256,64,64]{0,2,1:T(8,128)} fusion(f32[256,64,64]{0,2,1:T(8,128)S(1)} %fusion.29, f32[256,64,64]{0,1,2:T(8,128)S(1)} %get-tuple-element.14), kind=kOutput, calls=%fused_computation.54 | convolution fusion | flops 806412288 | bytes 12582912 | tf_op jit(solution)/shard_map/ckb,bm->ckm/dot_general | solution.py:37
  378.1 10.5 %multiply_add_fusion.1 = (f32[256,64,64]{0,2,1:T(8,128)S(1)}, f32[256,64,64]{0,2,1:T(8,128)S(1)}) fusion(f32[256,64,64]{0,2,1:T(8,128)S(1)} %fusion.47, f32[256,64,64]{0,2,1:T(8,128)} %fusion.41, f32[256,64,64]{0,2,1:T(8,128)} %fusion.50, f32[256,64,64]{0,2,1:T(8,128)} %fusion.27, f32[256,64,64]{0,1,2:T(8,128)S(1)} %get-tuple-element.14), kind=kOutput, calls=%fused_computation.20 | convolution fusion | flops 812703744 | bytes 29360128 | tf_op jit(solution)/shard_map/ckb,bm->ckm/dot_general | solution.py:40
  402.2 6.8 %multiply_subtract_fusion = (f32[256,64,64]{0,2,1:T(8,128)S(1)}, f32[256,64,64]{0,2,1:T(8,128)S(1)}) fusion(f32[256,64,64]{0,2,1:T(8,128)S(1)} %convolution_subtract_fusion, f32[64,64]{1,0:T(8,128)S(1)} %get-tuple-element.18, f32[64,64]{1,0:T(8,128)S(1)} %get-tuple-element.19, f32[256,64,64]{0,2,1:T(8,128)S(1)} %fusion.61, ...), kind=kOutput, calls=%fused_computation.19 | convolution fusion | flops 812703744 | bytes 21004288 | tf_op jit(solution)/shard_map/ckm,bm->ckb/dot_general | solution.py:52
  409.0 6.0 %fusion.9 = f32[64,256,64]{1,0,2:T(8,128)S(1)} fusion(f32[256,64,64]{0,2,1:T(8,128)S(1)} %get-tuple-element.8), kind=kOutput, calls=%fused_computation.13 | convolution fusion | flops 805363712 | bytes 8388608 | tf_op jit(solution)/shard_map/ckb,ak->cab/dot_general | solution.py:61
  415.1 6.4 %multiply_bitcast_fusion = f32[256,64,64]{0,1,2:T(8,128)S(1)} fusion(f32[64,256,64]{1,0,2:T(8,128)S(1)} %fusion.9, f32[256,64,64]{0,2,1:T(8,128)S(1)} %get-tuple-element.7), kind=kOutput, calls=%fused_computation.17 | convolution fusion | flops 807460864 | bytes 12582912 | tf_op jit(solution)/shard_map/ckb,ak->cab/dot_general | solution.py:61
  424.3 11.7 %copy.204 = bf16[1,256,2048]{1,0,2:T(2,128)(2,1)S(1)} copy(bf16[1,256,2048]{1,2,0:T(8,128)(2,1)S(1)} %fusion.57) | data formatting | bytes 2097152 | tf_op jit(solution)/shard_map/reshape | solution.py:135
  436.5 10.6 %reduce = bf16[2048,256]{1,0:T(8,128)(2,1)S(1)} reduce(bf16[2048,1,256]{2,1,0:T(2,128)(2,1)S(1)} %bitcast.137, bf16[]{:T(256)} %broadcast.298), dimensions={1}, to_apply=%bitcast.127.reduce_sub_computation | reduce | bytes 2097154
  447.5 17.1 %all_to_all.39 = bf16[4,2,65536]{2,1,0:T(2,128)(2,1)S(1)} all-to-all(bf16[4,2,65536]{2,1,0:T(2,128)(2,1)S(1)} %reshape.133), channel_id=1, replica_groups=mesh['groups'=2,'seq'=4,'chan'=4] {'seq'}, dimensions={0} | all-to-all | bytes 2097152 | tf_op jit(solution)/shard_map/all_to_all | solution.py:134
  470.3 80.9 %all-gather.8.cloned.1.call-done = bf16[4096,512]{0,1:T(8,128)(2,1)} async-done(((bf16[1024,512]{0,1:T(8,128)(2,1)}), bf16[4096,512]{0,1:T(8,128)(2,1)}) %all-gather.8.cloned.1.call-update) | async-done | bytes 4194320 | tf_op jit(solution)/shard_map/all_gather | solution.py:139
  551.2 10.1 %add_convert_fusion = bf16[512,1024]{1,0:T(8,128)(2,1)} fusion(bf16[512,1024]{1,0:T(8,128)(2,1)S(1)} %copy-done.3, bf16[4096,512]{0,1:T(8,128)(2,1)} %all-gather.8.cloned.1.call-done, bf16[4096,1024]{1,0:T(8,128)(2,1)} %param.13), kind=kOutput, calls=%fused_computation.67 | convolution fusion | flops 4296540160 | bytes 14680064 | tf_op jit(solution)/shard_map/dot_general | solution.py:140
  (55 shorter events, 53.7 us)
Async XLA Ops:
  6.5 85.9 %all-gather.4.cloned.1.call-start = ((), (), s32[]{:S(2)}) async-start(), calls=%async_computation.3 | async-start | bytes 5242880 | tf_op jit(solution)/shard_map/all_gather | solution.py:111
  7.3 240.0 %all-gather.6.cloned.1.call-start = ((), (), s32[]{:S(2)}) async-start(), calls=%async_computation.4 | async-start | bytes 31457280 | tf_op jit(solution)/shard_map/all_gather | solution.py:117
  8.0 239.3 %copy-start.5 = (f32[4096]{0:T(1024)S(1)}, f32[4096]{0:T(1024)}, u32[]{:S(2)}) copy-start(f32[4096]{0:T(1024)} %param.8) | copy-start | bytes 49156
  8.0 266.8 %all-to-all-start.1 = ((f32[1,4,256,512]{3,2,0,1:T(8,128)}), f32[1,4,256,512]{3,2,0,1:T(8,128)S(1)}, u32[]{:S(2)}, u32[]{:S(2)}) async-start(f32[1,4,256,512]{3,2,0,1:T(8,128)} %bitcast.143), calls=%async_computation.1 | async-start | bytes 4194304 | tf_op jit(solution)/shard_map/all_to_all | solution.py:123
  95.5 172.2 %copy-start.4 = (f32[3,3,1024]{2,1,0:T(4,128)S(1)}, f32[3,3,1024]{2,1,0:T(4,128)}, u32[]{:S(2)}) copy-start(f32[3,3,1024]{2,1,0:T(4,128)} %param.10) | copy-start | bytes 110596
  265.5 3.0 collective-permute-start
  271.5 1.6 copy-start.1
  274.8 6.2 %copy-start.2 = (f32[1,4,256,512]{3,2,0,1:T(8,128)}, f32[1,4,256,512]{3,2,0,1:T(8,128)S(1)}, u32[]{:S(2)}) copy-start(f32[1,4,256,512]{3,2,0,1:T(8,128)S(1)} %all-to-all-done.1) | copy-start | bytes 6291460
  274.9 30.2 %all-to-all-start = ((bf16[2,4,256,512]{2,3,0,1:T(8,128)(2,1)}), bf16[2,4,256,512]{2,3,0,1:T(8,128)(2,1)}, u32[]{:S(2)}, u32[]{:S(2)}) async-start(bf16[2,4,256,512]{2,3,0,1:T(8,128)(2,1)} %bitcast.136), calls=%async_computation | async-start | bytes 4194304 | tf_op jit(solution)/shard_map/all_to_all | solution.py:130
  279.3 271.9 %all-gather.8.cloned.1.call-start = ((), (), s32[]{:S(2)}) async-start(), calls=%async_computation.5 | async-start | bytes 5242880 | tf_op jit(solution)/shard_map/all_gather | solution.py:139
  307.3 1.9 copy-start
  467.2 84.0 %copy-start.3 = (bf16[512,1024]{1,0:T(8,128)(2,1)S(1)}, bf16[512,1024]{1,0:T(8,128)(2,1)}, u32[]{:S(2)}) copy-start(bf16[512,1024]{1,0:T(8,128)(2,1)} %param.7) | copy-start | bytes 3145732
Sparse Core Ops, SparseCore 0:
  8.9 83.4 all-gather.3
  94.0 153.2 all-gather.5
  470.5 80.7 all-gather.7
where the time goes:
time: 574 us; the launch traced here: 568 us
  waiting for transfers between devices  322 us (56%)
  matrix products  155 us (27%)
  local copies, waits for them, and re-layouts  28.4 us (5%)
  other arithmetic  20.5 us (4%)
  blocking collectives  17.1 us (3%)
  between operations  13.7 us (2%)
  starting transfers between devices  11.4 us (2%)
    all_gather x1, waiting for transfers between devices, body(): lax.all_gather(proj_weight, 'seq', axis=0, tiled=True)  152 us
    all_gather x1, waiting for transfers between devices, body(): full_mix = lax.all_gather(gated, 'chan', axis=0, tiled=True)  80.9 us
    all_gather x1, waiting for transfers between devices, body(): whole = lax.all_gather(tokens, 'chan', axis=1, tiled=True)  80.1 us
    dot_general x2, matrix products, forward_spectrum(): part_re = jnp.einsum('cab,ak->ckb', grid_rows, cos_first, precision=HIGHEST)  19.7 us
    dot_general x1, matrix products, body(): lax.dot_general(lax.all_gather(proj_weight, 'seq', axis=0, tiled=True), r...  18.2 us
    dot_general x2, matrix products, forward_spectrum(): jnp.einsum('ckb,bm->ckm', part_re, sin_second, precision=HIGHEST)  17.9 us
    all_to_all x1, blocking collectives, body(): lax.all_to_all(result.reshape(1, subset, length), 'seq', split_axis=2, co...  17.1 us
    dot_general x2, matrix products, forward_spectrum(): jnp.einsum('ckb,bm->ckm', part_re, cos_second, precision=HIGHEST)  14.6 us
  transfers between devices with their start and end apart: 6, of which 5 were waited for; matrix products, arithmetic and copies ran while one was open for 8% of the time, Pallas kernels for 0%

commit v1 on v0

--- a/solution.py
+++ b/solution.py
@@ -136,7 +136,12 @@
     )
     returned = returned.reshape(local_chan, local_rows)
     gated = (featured[0].astype(jnp.float32) * returned.astype(jnp.float32)).astype(jnp.bfloat16)
-    full_mix = lax.all_gather(gated, "chan", axis=0, tiled=True)
+    ring = [gated]
+    for hop in range(3):
+        ring.append(lax.ppermute(ring[-1], "chan", [(dev, (dev + 1) % 4) for dev in range(4)]))
+    full_mix = jnp.roll(
+        jnp.concatenate(ring[::-1], axis=0), (lax.axis_index("chan") + 1) * ring[0].shape[0], axis=0
+    )
     update = lax.dot_general(
         full_mix, out_weight, (((0,), (0,)), ((), ())), preferred_element_type=jnp.float32
     )

time: 574 us -> 570 us (level)
    all_gather x1 -> x0, waiting for transfers between devices: 80.9 us -> none  [body(): full_mix = lax.all_gather(gated, 'chan', axis=0, tiled=True)]
    ppermute x0 -> x3, waiting for transfers between devices: none -> 75 us  [body(): lax.ppermute(ring[-1], 'chan', [(dev, (dev + 1) % 4) for dev in range(4)])]
  transfers between devices with their start and end apart: 6 -> 8, of which waited for: 5 -> 7; matrix products, arithmetic and copies ran while one was open for 8% -> 8% of each run, Pallas kernels for 0% -> 0%
where the time goes in v1:
time: 570 us; the launch traced here: 565 us
  waiting for transfers between devices  317 us (56%)
  matrix products  153 us (27%)
  local copies, waits for them, and re-layouts  31.5 us (6%)
  other arithmetic  19.5 us (3%)
  blocking collectives  17.1 us (3%)
  between operations  14 us (2%)
  starting transfers between devices  12.9 us (2%)
    all_gather x1, waiting for transfers between devices, body(): lax.all_gather(proj_weight, 'seq', axis=0, tiled=True)  152 us
    all_gather x1, waiting for transfers between devices, body(): whole = lax.all_gather(tokens, 'chan', axis=1, tiled=True)  80.1 us
    ppermute x3, waiting for transfers between devices, body(): lax.ppermute(ring[-1], 'chan', [(dev, (dev + 1) % 4) for dev in range(4)])  75 us
    dot_general x2, matrix products, forward_spectrum(): part_re = jnp.einsum('cab,ak->ckb', grid_rows, cos_first, precision=HIGHEST)  19.7 us
    dot_general x1, matrix products, body(): lax.dot_general(lax.all_gather(proj_weight, 'seq', axis=0, tiled=True), r...  18.2 us
    dot_general x2, matrix products, forward_spectrum(): jnp.einsum('ckb,bm->ckm', part_re, sin_second, precision=HIGHEST)  17.9 us
    all_to_all x1, blocking collectives, body(): lax.all_to_all(result.reshape(1, subset, length), 'seq', split_axis=2, co...  17.1 us
    dot_general x2, matrix products, forward_spectrum(): jnp.einsum('ckb,bm->ckm', part_re, cos_second, precision=HIGHEST)  14.6 us
  transfers between devices with their start and end apart: 8, of which 7 were waited for; matrix products, arithmetic and copies ran while one was open for 8% of the time, Pallas kernels for 0%

profile of v1, /device:TPU:0, one launch (start us, length us, event | category | flops | bytes accessed | tf_op | source)
XLA Modules:
  0.0 564.7 jit_solution(9745556257955648758)
XLA Ops:
  12.3 80.1 %all-gather.3.cloned.1.call-done = bf16[512,4096]{1,0:T(8,128)(2,1)} async-done(((bf16[512,1024]{1,0:T(8,128)(2,1)}), bf16[512,4096]{1,0:T(8,128)(2,1)}) %all-gather.3.cloned.1.call-update) | async-done | bytes 4194320 | tf_op jit(solution)/shard_map/all_gather | solution.py:111
  95.5 151.8 %all-gather.5.cloned.1.call-done = bf16[4096,3,1024]{2,0,1:T(8,128)(2,1)} async-done(((bf16[1024,3,1024]{2,0,1:T(8,128)(2,1)}), bf16[4096,3,1024]{2,0,1:T(8,128)(2,1)}) %all-gather.5.cloned.1.call-update) | async-done | bytes 25165840 | tf_op jit(solution)/shard_map/all_gather | solution.py:117
  247.3 18.2 %convert_bitcast_fusion = bf16[3,1024,512]{1,2,0:T(8,128)(2,1)S(1)} fusion(bf16[4096,3,1024]{2,0,1:T(8,128)(2,1)} %all-gather.5.cloned.1.call-done, bf16[512,4096]{1,0:T(8,128)(2,1)} %all-gather.3.cloned.1.call-done, f32[4096]{0:T(1024)S(1)} %copy-done.5, f32[512]{0:T(512)S(1)} %add_rsqrt_fusion), kind=kOutput, calls=%fused_computation.55 | convolution fusion | flops 12894863360 | bytes 32524288 | tf_op jit(solution)/shard_map/dot_general | solution.py:116
  283.4 7.2 %fusion.25 = f32[64,256,64]{1,0,2:T(8,128)} fusion(f32[256,64,64]{0,2,1:T(8,128)S(1)} %bitcast.127), kind=kOutput, calls=%fused_computation.38 | convolution fusion | flops 805363712 | bytes 8388608 | tf_op jit(solution)/shard_map/cab,ak->ckb/dot_general | solution.py:30
  290.5 7.2 %fusion.27 = f32[64,256,64]{1,0,2:T(8,128)} fusion(f32[256,64,64]{0,2,1:T(8,128)S(1)} %bitcast.128), kind=kOutput, calls=%fused_computation.40 | convolution fusion | flops 805363712 | bytes 8388608 | tf_op jit(solution)/shard_map/cab,ak->ckb/dot_general | solution.py:29
  297.7 7.8 %all-to-all-done = bf16[2,4,256,512]{2,3,0,1:T(8,128)(2,1)} async-done(((bf16[2,4,256,512]{2,3,0,1:T(8,128)(2,1)}), bf16[2,4,256,512]{2,3,0,1:T(8,128)(2,1)}, u32[]{:S(2)}, u32[]{:S(2)}) %all-to-all-start) | async-done | bytes 2097184 | tf_op jit(solution)/shard_map/all_to_all | solution.py:130
  309.7 7.1 %fusion.37 = f32[64,256,64]{1,0,2:T(8,128)} fusion(f32[256,64,64]{0,2,1:T(8,128)S(1)} %bitcast.129), kind=kOutput, calls=%fused_computation.50 | convolution fusion | flops 805363712 | bytes 8388608 | tf_op jit(solution)/shard_map/cab,ak->ckb/dot_general | solution.py:30
  316.8 12.5 %subtract_bitcast_fusion = (f32[256,64,64]{0,1,2:T(8,128)S(1)}, f32[256,64,64]{0,1,2:T(8,128)S(1)}, f32[256,64,64]{0,1,2:T(8,128)S(1)}, f32[256,64,64]{0,1,2:T(8,128)S(1)}) fusion(f32[64,256,64]{1,0,2:T(8,128)} %fusion.25, f32[64,256,64]{1,0,2:T(8,128)} %fusion.27, f32[64,64]{0,1:T(8,128)S(1)} %copy.102, f32[64,64]{0,1:T(8,128)S(1)} %copy.99, ...), kind=kOutput, calls=%fused_computation.25 | convolution fusion | flops 817946624 | bytes 33587200 | tf_op jit(solution)/shard_map/cab,ak->ckb/dot_general | solution.py:29
  329.3 6.5 %fusion.17 = f32[256,64,64]{0,2,1:T(8,128)S(1)} fusion(f32[256,64,64]{0,1,2:T(8,128)S(1)} %get-tuple-element.10), kind=kOutput, calls=%fused_computation.30 | convolution fusion | flops 805363712 | bytes 8388608 | tf_op jit(solution)/shard_map/ckb,bm->ckm/dot_general | solution.py:40
  335.8 6.9 %fusion.19 = f32[256,64,64]{0,2,1:T(8,128)S(1)} fusion(f32[256,64,64]{0,1,2:T(8,128)S(1)} %get-tuple-element.10), kind=kOutput, calls=%fused_computation.32 | convolution fusion | flops 805363712 | bytes 8388608 | tf_op jit(solution)/shard_map/ckb,bm->ckm/dot_general | solution.py:37
  342.7 7.3 %fusion.29 = f32[256,64,64]{0,2,1:T(8,128)} fusion(f32[256,64,64]{0,1,2:T(8,128)S(1)} %get-tuple-element.13), kind=kOutput, calls=%fused_computation.42 | convolution fusion | flops 805363712 | bytes 8388608 | tf_op jit(solution)/shard_map/ckb,bm->ckm/dot_general | solution.py:40
  350.0 6.5 %fusion.31 = f32[256,64,64]{0,2,1:T(8,128)S(1)} fusion(f32[256,64,64]{0,1,2:T(8,128)S(1)} %get-tuple-element.13), kind=kOutput, calls=%fused_computation.44 | convolution fusion | flops 805363712 | bytes 8388608 | tf_op jit(solution)/shard_map/ckb,bm->ckm/dot_general | solution.py:37
  356.5 7.3 %fusion.49 = f32[256,64,64]{0,2,1:T(8,128)S(1)} fusion(f32[256,64,64]{0,2,1:T(8,128)S(1)} %fusion.19, f32[256,64,64]{0,1,2:T(8,128)S(1)} %get-tuple-element.9), kind=kOutput, calls=%fused_computation.58 | convolution fusion | flops 806412288 | bytes 12582912 | tf_op jit(solution)/shard_map/ckb,bm->ckm/dot_general | solution.py:37
  363.8 7.4 %fusion.52 = f32[256,64,64]{0,2,1:T(8,128)} fusion(f32[256,64,64]{0,2,1:T(8,128)S(1)} %fusion.17, f32[256,64,64]{0,1,2:T(8,128)S(1)} %get-tuple-element.9), kind=kOutput, calls=%fused_computation.59 | convolution fusion | flops 806412288 | bytes 12582912 | tf_op jit(solution)/shard_map/ckb,bm->ckm/dot_general | solution.py:40
  371.1 7.4 %fusion.43 = f32[256,64,64]{0,2,1:T(8,128)} fusion(f32[256,64,64]{0,2,1:T(8,128)S(1)} %fusion.31, f32[256,64,64]{0,1,2:T(8,128)S(1)} %get-tuple-element.14), kind=kOutput, calls=%fused_computation.56 | convolution fusion | flops 806412288 | bytes 12582912 | tf_op jit(solution)/shard_map/ckb,bm->ckm/dot_general | solution.py:37
  378.5 10.5 %multiply_add_fusion.1 = (f32[256,64,64]{0,2,1:T(8,128)S(1)}, f32[256,64,64]{0,2,1:T(8,128)S(1)}) fusion(f32[256,64,64]{0,2,1:T(8,128)S(1)} %fusion.49, f32[256,64,64]{0,2,1:T(8,128)} %fusion.43, f32[256,64,64]{0,2,1:T(8,128)} %fusion.52, f32[256,64,64]{0,2,1:T(8,128)} %fusion.29, f32[256,64,64]{0,1,2:T(8,128)S(1)} %get-tuple-element.14), kind=kOutput, calls=%fused_computation.22 | convolution fusion | flops 812703744 | bytes 29360128 | tf_op jit(solution)/shard_map/ckb,bm->ckm/dot_general | solution.py:40
  402.7 6.8 %multiply_subtract_fusion = (f32[256,64,64]{0,2,1:T(8,128)S(1)}, f32[256,64,64]{0,2,1:T(8,128)S(1)}) fusion(f32[256,64,64]{0,2,1:T(8,128)S(1)} %convolution_subtract_fusion, f32[64,64]{1,0:T(8,128)S(1)} %get-tuple-element.18, f32[64,64]{1,0:T(8,128)S(1)} %get-tuple-element.19, f32[256,64,64]{0,2,1:T(8,128)S(1)} %fusion.65, ...), kind=kOutput, calls=%fused_computation.21 | convolution fusion | flops 812703744 | bytes 21004288 | tf_op jit(solution)/shard_map/ckm,bm->ckb/dot_general | solution.py:52
  424.7 11.7 %copy.204 = bf16[1,256,2048]{1,0,2:T(2,128)(2,1)S(1)} copy(bf16[1,256,2048]{1,2,0:T(8,128)(2,1)S(1)} %fusion.61) | data formatting | bytes 2097152 | tf_op jit(solution)/shard_map/reshape | solution.py:135
  437.0 10.6 %reduce = bf16[2048,256]{1,0:T(8,128)(2,1)S(1)} reduce(bf16[2048,1,256]{2,1,0:T(2,128)(2,1)S(1)} %bitcast.136, bf16[]{:T(256)} %broadcast.299), dimensions={1}, to_apply=%bitcast.126.reduce_sub_computation | reduce | bytes 2097154
  447.9 17.1 %all_to_all.39 = bf16[4,2,65536]{2,1,0:T(2,128)(2,1)S(1)} all-to-all(bf16[4,2,65536]{2,1,0:T(2,128)(2,1)S(1)} %reshape.133), channel_id=1, replica_groups=mesh['groups'=2,'seq'=4,'chan'=4] {'seq'}, dimensions={0} | all-to-all | bytes 2097152 | tf_op jit(solution)/shard_map/all_to_all | solution.py:134
  471.3 24.8 %collective-permute-done.1 = bf16[1024,512]{0,1:T(8,128)(2,1)S(1)} collective-permute-done((bf16[1024,512]{0,1:T(8,128)(2,1)S(1)}, bf16[1024,512]{0,1:T(8,128)(2,1)S(1)}, u32[]{:S(2)}, u32[]{:S(2)}) %collective-permute-start.1) | collective-permute-done | bytes 1048608 | tf_op jit(solution)/shard_map/ppermute | solution.py:141
  496.2 25.5 %collective-permute-done.2 = bf16[1024,512]{0,1:T(8,128)(2,1)S(1)} collective-permute-done((bf16[1024,512]{0,1:T(8,128)(2,1)S(1)}, bf16[1024,512]{0,1:T(8,128)(2,1)S(1)}, u32[]{:S(2)}, u32[]{:S(2)}) %collective-permute-start.2) | collective-permute-done | bytes 1048608 | tf_op jit(solution)/shard_map/ppermute | solution.py:141
  521.6 24.7 %collective-permute-done.3 = bf16[1024,512]{0,1:T(8,128)(2,1)} collective-permute-done((bf16[1024,512]{0,1:T(8,128)(2,1)S(1)}, bf16[1024,512]{0,1:T(8,128)(2,1)}, u32[]{:S(2)}, u32[]{:S(2)}) %collective-permute-start.3) | collective-permute-done | bytes 1048608 | tf_op jit(solution)/shard_map/ppermute | solution.py:141
  549.5 8.1 %add_convert_fusion = bf16[512,1024]{1,0:T(8,128)(2,1)} fusion(bf16[512,1024]{1,0:T(8,128)(2,1)S(1)} %copy-done.3, bf16[4096,1024]{1,0:T(8,128)(2,1)} %param.13, bf16[8192,512]{0,1:T(8,128)(2,1)S(1)} %constant_dynamic-update-slice_fusion, s32[]{:T(128)S(6)} %select_n.113), kind=kOutput, calls=%fused_computation.69 | convolution fusion | flops 4296540160 | bytes 14680068 | tf_op jit(solution)/shard_map/dot_general | solution.py:145
  (66 shorter events, 69.8 us)
Async XLA Ops:
  6.5 85.9 %all-gather.3.cloned.1.call-start = ((), (), s32[]{:S(2)}) async-start(), calls=%async_computation.3 | async-start | bytes 5242880 | tf_op jit(solution)/shard_map/all_gather | solution.py:111
  7.3 240.0 %all-gather.5.cloned.1.call-start = ((), (), s32[]{:S(2)}) async-start(), calls=%async_computation.4 | async-start | bytes 31457280 | tf_op jit(solution)/shard_map/all_gather | solution.py:117
  8.0 239.3 %copy-start.5 = (f32[4096]{0:T(1024)S(1)}, f32[4096]{0:T(1024)}, u32[]{:S(2)}) copy-start(f32[4096]{0:T(1024)} %param.8) | copy-start | bytes 49156
  8.0 266.8 %all-to-all-start.1 = ((f32[1,4,256,512]{3,2,0,1:T(8,128)}), f32[1,4,256,512]{3,2,0,1:T(8,128)S(1)}, u32[]{:S(2)}, u32[]{:S(2)}) async-start(f32[1,4,256,512]{3,2,0,1:T(8,128)} %bitcast.142), calls=%async_computation.1 | async-start | bytes 4194304 | tf_op jit(solution)/shard_map/all_to_all | solution.py:123
  95.5 172.2 %copy-start.4 = (f32[3,3,1024]{2,1,0:T(4,128)S(1)}, f32[3,3,1024]{2,1,0:T(4,128)}, u32[]{:S(2)}) copy-start(f32[3,3,1024]{2,1,0:T(4,128)} %param.10) | copy-start | bytes 110596
  265.5 3.0 collective-permute-start
  271.5 1.6 copy-start.1
  274.8 6.1 %copy-start.2 = (f32[1,4,256,512]{3,2,0,1:T(8,128)}, f32[1,4,256,512]{3,2,0,1:T(8,128)S(1)}, u32[]{:S(2)}) copy-start(f32[1,4,256,512]{3,2,0,1:T(8,128)S(1)} %all-to-all-done.1) | copy-start | bytes 6291460
  274.9 30.6 %all-to-all-start = ((bf16[2,4,256,512]{2,3,0,1:T(8,128)(2,1)}), bf16[2,4,256,512]{2,3,0,1:T(8,128)(2,1)}, u32[]{:S(2)}, u32[]{:S(2)}) async-start(bf16[2,4,256,512]{2,3,0,1:T(8,128)(2,1)} %bitcast.135), calls=%async_computation | async-start | bytes 4194304 | tf_op jit(solution)/shard_map/all_to_all | solution.py:130
  307.7 1.9 copy-start
  469.8 26.4 %collective-permute-start.1 = (bf16[1024,512]{0,1:T(8,128)(2,1)S(1)}, bf16[1024,512]{0,1:T(8,128)(2,1)S(1)}, u32[]{:S(2)}, u32[]{:S(2)}) collective-permute-start(bf16[1024,512]{0,1:T(8,128)(2,1)S(1)} %fusion.58), channel_id=1, source_target_pairs={{0,1},{1,2},{2,3},{3,0},{4,5},{5,6},{6,7},{7,4},{8,9},{9,10},{10,1... | collective-permute-start | bytes 3145736 | tf_op jit(solution)/shard_map/ppermute | solution.py:141
  496.2 25.5 %collective-permute-start.2 = (bf16[1024,512]{0,1:T(8,128)(2,1)S(1)}, bf16[1024,512]{0,1:T(8,128)(2,1)S(1)}, u32[]{:S(2)}, u32[]{:S(2)}) collective-permute-start(bf16[1024,512]{0,1:T(8,128)(2,1)S(1)} %collective-permute-done.1), channel_id=1, source_target_pairs={{0,1},{1,2},{2,3},{3,0},{4,5},{5,6},{6,7},{7,4},{8,9},{9,10},{10,1... | collective-permute-start | bytes 3145736 | tf_op jit(solution)/shard_map/ppermute | solution.py:141
  521.6 24.7 %collective-permute-start.3 = (bf16[1024,512]{0,1:T(8,128)(2,1)S(1)}, bf16[1024,512]{0,1:T(8,128)(2,1)}, u32[]{:S(2)}, u32[]{:S(2)}) collective-permute-start(bf16[1024,512]{0,1:T(8,128)(2,1)S(1)} %collective-permute-done.2), channel_id=1, source_target_pairs={{0,1},{1,2},{2,3},{3,0},{4,5},{5,6},{6,7},{7,4},{8,9},{9,10},{10,1... | collective-permute-start | bytes 3145736 | tf_op jit(solution)/shard_map/ppermute | solution.py:141
  547.9 1.6 copy-start.3
Sparse Core Ops, SparseCore 0:
  8.9 83.4 all-gather.2
  94.0 153.2 all-gather.4
